TPU v7x, 32 devices: a whole 2x2x4 slice. The times are simulated.
32 devices in a mesh: aux: 4 (over x, core), orb: 8 (over z, y).
Axes of the slice: x: 2, y: 2, z: 4, core: 2. Of those that a mesh axis runs over, the one named last changes fastest.
Arguments:
- three_center: bfloat16 [640, 8, 3, 4096], P(('aux', 'orb')), may hold values from -1.5 to 1.5
- atom_size: int32 [8], replicated, may hold values from 32 to 64
- tensor_pattern: int32 [40, 8, 3], P('aux', 'orb'), may hold values 0 or 1
- green_occ: bfloat16 [8, 3, 4096], P('orb'), may hold values from -0.5 to 0.5
- green_virt: bfloat16 [8, 3, 4096], P('orb'), may hold values from -0.5 to 0.5
- green_pattern: int32 [8, 3], P('orb'), may hold values 0 or 1
Outputs:
- chi: float32 [640, 640], P(('aux', 'orb'))
Inputs may be any that keep to these rules, and one draw needn't show every extreme that they name: `atom_size`: functions in use per block.
All inputs are finite; a program needn't handle non-finite values. No bound on the sum of `tensor_pattern` or of `green_pattern` on one device may be relied on, other than what follows from the above.
Results may differ from a plain program's by a relative error of at most 0.0041.
Values may be sent and summed in bfloat16 or wider, within the bound.
A program may use at most 128 MiB of HBM per device.

v0:
```python
import jax
import jax.numpy as jnp
from jax import lax
from jax.sharding import PartitionSpec as P

BS = 64
R = 1
W = 3
ABS = 16


def padded(block, sides, width):
    for axis, dim in sides:
        count = lax.axis_size(axis)
        forward = [(i, i + 1) for i in range(count - 1)]
        backward = [(target, source) for source, target in forward]
        low = lax.ppermute(
            lax.slice_in_dim(block, block.shape[dim] - width, None, axis=dim), axis, forward
        )
        high = lax.ppermute(lax.slice_in_dim(block, 0, width, axis=dim), axis, backward)
        block = jnp.concatenate([low, block, high], axis=dim)
    return block


def block_masks(atom_size, first_block, local_blocks):
    total_blocks = atom_size.shape[0]
    owned = first_block + jnp.arange(local_blocks, dtype=jnp.int32)
    offsets = jnp.arange(W, dtype=jnp.int32)
    partner = owned[:, None] + offsets[None, :] - R
    inside = (partner >= 0) & (partner < total_blocks)
    catalog = jnp.arange(total_blocks, dtype=jnp.int32)
    size_partner = jnp.sum(jnp.where(partner[:, :, None] == catalog, atom_size, 0), axis=2)
    size_owned = jnp.sum(jnp.where(owned[:, None] == catalog, atom_size, 0), axis=1)
    funcs = jnp.arange(BS, dtype=jnp.int32)
    rows_ok = (funcs[None, None, :] < size_partner[:, :, None]) & inside[:, :, None]
    cols_ok = funcs[None, :] < size_owned[:, None]
    pair_ok = rows_ok[:, :, :, None] & cols_ok[:, None, None, :]
    return (inside, pair_ok.reshape(local_blocks, W, BS * BS))


def first_products(padded_occ, tensor):
    rows = tensor.shape[0]
    local_blocks = tensor.shape[1]
    results = []
    for target in range(W):
        total = jnp.zeros((rows, local_blocks, BS, BS), jnp.float32)
        for source in range(W):
            if abs(target - source) <= R:
                green = padded_occ[source : source + local_blocks, target - source + R].reshape(
                    local_blocks, BS, BS
                )
                block = tensor[:, :, source].reshape(rows, local_blocks, BS, BS)
                total = total + jnp.einsum(
                    "nlm,pnmv->pnlv", green, block, preferred_element_type=jnp.float32
                )
        results.append(total.astype(jnp.bfloat16).reshape(rows, local_blocks, BS * BS))
    return jnp.concatenate(results, axis=2).reshape(rows, local_blocks * W * BS * BS)


def second_products(padded_tensor, virt):
    rows = padded_tensor.shape[0]
    local_blocks = virt.shape[0]
    results = []
    for target in range(W):
        total = jnp.zeros((rows, local_blocks, BS, BS), jnp.float32)
        for source in range(W):
            if abs(target - source) <= R:
                block = padded_tensor[
                    :, source : source + local_blocks, target - source + R
                ].reshape(rows, local_blocks, BS, BS)
                green = virt[:, source].reshape(local_blocks, BS, BS)
                total = total + jnp.einsum(
                    "pnls,nsv->pnlv", block, green, preferred_element_type=jnp.float32
                )
        results.append(total.astype(jnp.bfloat16).reshape(rows, local_blocks, BS * BS))
    return jnp.concatenate(results, axis=2).reshape(rows, local_blocks * W * BS * BS)


def body(three_center, atom_size, tensor_pattern, green_occ, green_virt, green_pattern):
    regrouped = lax.all_to_all(three_center, "orb", split_axis=1, concat_axis=0, tiled=True)
    local_blocks = regrouped.shape[1]
    first_block = lax.axis_index("orb") * local_blocks
    inside, pair_ok = block_masks(atom_size, first_block, local_blocks)
    pattern_rows = jnp.repeat(tensor_pattern, ABS, axis=0)
    keep = (pattern_rows[..., None] > 0) & pair_ok[None]
    tensor = jnp.where(keep, regrouped, jnp.zeros((), regrouped.dtype))
    diagonal = jnp.arange(W, dtype=jnp.int32) == R
    green_keep = ((green_pattern > 0) | diagonal[None, :]) & inside
    green_mask = green_keep[..., None] & pair_ok
    occ = jnp.where(green_mask, green_occ, jnp.zeros((), green_occ.dtype))
    virt = jnp.where(green_mask, green_virt, jnp.zeros((), green_virt.dtype))
    padded_occ = padded(occ, (("orb", 0),), R)
    padded_tensor = padded(tensor, (("orb", 1),), R)
    first = first_products(padded_occ, tensor)
    second = second_products(padded_tensor, virt)
    left_all, right_all = (
        lax.all_to_all(first, "aux", split_axis=1, concat_axis=0, tiled=True),
        lax.all_to_all(second, "aux", split_axis=1, concat_axis=0, tiled=True),
    )
    row_sums = lax.psum_scatter(
        lax.dot_general(
            left_all, right_all, (((1,), (1,)), ((), ())), preferred_element_type=jnp.float32
        ),
        "aux",
        scatter_dimension=0,
        tiled=True,
    )
    return lax.psum_scatter(row_sums, "orb", scatter_dimension=0, tiled=True)


def solution(mesh):
    return jax.shard_map(
        body,
        mesh=mesh,
        in_specs=(
            P(("aux", "orb"), None, None, None),
            P(),
            P("aux", "orb", None),
            P("orb", None, None),
            P("orb", None, None),
            P("orb", None),
        ),
        out_specs=P(("aux", "orb"), None),
        check_vma=False,
    )
```

profile of v0, /device:TPU:0, one launch (start us, length us, event | category | flops | bytes accessed | tf_op | source)
XLA Modules:
  0.0 547.4 jit_solution(12280116020150700102)
XLA Ops:
  6.5 6.5 %copy.128 = bf16[20,8,3,4096]{3,0,2,1:T(8,128)(2,1)} copy(bf16[20,8,3,4096]{3,1,2,0:T(8,128)(2,1)} %param.6) | data formatting | bytes 7864320 | tf_op args[0]
  13.1 7.5 %all-to-all-start = ((bf16[20,8,3,4096]{3,0,2,1:T(8,128)(2,1)}), bf16[20,8,3,4096]{3,0,2,1:T(8,128)(2,1)}, u32[]{:S(2)}, u32[]{:S(2)}) async-start(bf16[20,8,3,4096]{3,0,2,1:T(8,128)(2,1)} %copy.128), calls=%async_computation | async-start | bytes 9437184 | tf_op jit(solution)/shard_map/all_to_all | solution.py:80
  21.7 0.6 iota_compare_fusion.1
  22.6 3.9 collective-permute-start
  26.5 1.3 collective-permute-start.1
  28.9 30.9 %collective-permute-done = bf16[1,3,4096]{2,1,0:T(4,128)(2,1)S(1)} collective-permute-done((bf16[1,3,4096]{2,1,0:T(4,128)(2,1)S(1)}, bf16[1,3,4096]{2,1,0:T(4,128)(2,1)S(1)}, u32[]{:S(2)}, u32[]{:S(2)}) %collective-permute-start) | collective-permute-done | bytes 24608 | tf_op jit(solution)/shard_map/ppermute | solution.py:17
  60.3 65.1 %all-to-all-done = bf16[20,8,3,4096]{3,0,2,1:T(8,128)(2,1)} async-done(((bf16[20,8,3,4096]{3,0,2,1:T(8,128)(2,1)}), bf16[20,8,3,4096]{3,0,2,1:T(8,128)(2,1)}, u32[]{:S(2)}, u32[]{:S(2)}) %all-to-all-start) | async-done | bytes 3932192 | tf_op jit(solution)/shard_map/all_to_all | solution.py:80
  125.4 5.1 copy.129
  130.5 6.1 %all_to_all.44 = bf16[160,1,3,4096]{3,0,2,1:T(8,128)(2,1)} reshape(bf16[8,20,1,3,4096]{4,1,0,3,2:T(8,128)(2,1)} %copy.129) | data formatting | bytes 7864320 | tf_op jit(solution)/shard_map/all_to_all | solution.py:80
  136.5 5.5 and_select_fusion
  142.0 3.6 fusion.25
  145.6 5.0 collective-permute-start.2
  150.5 1.7 collective-permute-start.3
  152.3 4.8 reshape.442
  157.1 3.9 reshape.440
  161.0 3.9 reshape.447
  164.8 5.6 %copy.131 = bf16[160,64,64]{0,1,2:T(8,128)(2,1)S(1)} copy(bf16[160,64,64]{2,1,0:T(8,128)(2,1)} %reshape.442) | data formatting | bytes 2621440 | tf_op jit(solution)/shard_map/reshape.26
  170.4 6.7 %copy.130 = bf16[160,64,64]{0,1,2:T(8,128)(2,1)} copy(bf16[160,64,64]{2,1,0:T(8,128)(2,1)} %reshape.440) | data formatting | bytes 2621440 | tf_op jit(solution)/shard_map/reshape.23
  177.1 6.6 %copy.135 = bf16[160,64,64]{0,1,2:T(8,128)(2,1)} copy(bf16[160,64,64]{2,1,0:T(8,128)(2,1)} %reshape.447) | data formatting | bytes 2621440 | tf_op jit(solution)/shard_map/reshape.35
  183.8 0.7 fusion.29
  184.4 0.9 copy-done.3
  185.4 0.7 fusion.28
  186.0 0.9 copy-done.4
  186.9 2.0 fusion.6
  189.0 2.7 fusion.27
  191.7 6.2 %copy.136 = bf16[160,1,64,64]{3,2,0,1:T(8,128)(2,1)} copy(bf16[160,1,64,64]{0,2,3,1:T(8,128)(2,1)} %fusion.6) | data formatting | bytes 2621440 | tf_op jit(solution)/shard_map/convert_element_type | solution.py:56
  198.0 4.7 reshape.449
  202.6 4.8 fusion.7
  207.4 6.4 %copy.132 = bf16[160,1,64,64]{3,2,0,1:T(8,128)(2,1)} copy(bf16[160,1,64,64]{0,2,3,1:T(8,128)(2,1)} %fusion.7) | data formatting | bytes 2621440 | tf_op jit(solution)/shard_map/convert_element_type | solution.py:56
  213.8 4.7 reshape.444
  218.5 0.7 fusion.30
  219.2 0.9 copy-done.5
  220.1 2.1 fusion.8
  222.2 5.3 copy.139
  227.5 2.9 reshape.452
  230.4 3.6 pad_maximum_fusion
  234.0 9.0 %all_to_all.45 = bf16[160,4,3072]{2,1,0:T(4,128)(2,1)} reshape(bf16[160,1,12288]{2,0,1:T(8,128)(2,1)} %pad_maximum_fusion) | data formatting | bytes 7864320 | tf_op jit(solution)/shard_map/all_to_all | solution.py:97
  242.9 5.2 copy.140
  248.1 5.2 all-to-all-start.1
  253.6 4.8 fusion.2
  258.4 4.8 fusion.4
  263.2 4.8 fusion
  268.1 48.6 %collective-permute-done.2 = bf16[160,1,3,4096]{3,0,2,1:T(8,128)(2,1)} collective-permute-done((bf16[160,1,3,4096]{3,0,2,1:T(8,128)(2,1)}, bf16[160,1,3,4096]{3,0,2,1:T(8,128)(2,1)}, u32[]{:S(2)}, u32[]{:S(2)}) %collective-permute-start.2) | collective-permute-done | bytes 3932192 | tf_op jit(solution)/shard_map/ppermute | solution.py:17
  316.6 3.0 fusion.23
  319.7 3.3 copy.145
  323.0 3.6 fusion.24
  326.6 2.7 fusion.17
  329.3 3.1 copy.149
  332.4 5.6 %add_convert_fusion.1 = bf16[64,160,64]{1,0,2:T(8,128)(2,1)} fusion(f32[64,160,64]{1,0,2:T(8,128)} %fusion.17, f32[64,160,64]{1,0,2:T(8,128)} %fusion.2, bf16[160,64,64]{0,2,1:T(8,128)(2,1)S(1)} %bitcast.122, bf16[64,64]{1,0:T(8,128)(2,1)S(1)} %reshape.458), kind=kOutput, calls=%fused_computation.2 | convolution fusion | flops 85852160 | bytes 7872512 | tf_op jit(solution)/shard_map/pnls,nsv->pnlv/dot_general | solution.py:72
  338.0 3.8 copy.156
  341.8 1.8 copy.141
  343.6 4.2 add_convert_fusion.2
  347.9 3.9 copy.155
  351.8 1.8 copy.153
  353.6 4.3 add_convert_fusion
  357.9 4.0 copy.157
  361.9 3.1 pad_maximum_fusion.1
  365.0 9.0 %all_to_all.49 = bf16[160,4,3072]{2,1,0:T(4,128)(2,1)} reshape(bf16[160,1,12288]{2,0,1:T(8,128)(2,1)} %pad_maximum_fusion.1) | data formatting | bytes 7864320 | tf_op jit(solution)/shard_map/all_to_all | solution.py:98
  373.9 5.2 copy.158
  379.1 49.1 %all_to_all.56 = bf16[160,4,3072]{2,0,1:T(8,128)(2,1)S(1)} all-to-all(bf16[160,4,3072]{2,0,1:T(8,128)(2,1)} %copy.158), channel_id=1, replica_groups=mesh['aux'=4,'orb'=8] {'aux'}, dimensions={1} | all-to-all | bytes 7864320 | tf_op jit(solution)/shard_map/all_to_all | solution.py:98
  428.2 6.6 %fusion.26 = f32[640,640]{1,0:T(8,128)} fusion(bf16[640,3072]{1,0:T(8,128)(2,1)} %bitcast.10, bf16[640,3072]{1,0:T(8,128)(2,1)S(1)} %bitcast.128), kind=kOutput, calls=%fused_computation.57 | convolution fusion | flops 2516582400 | bytes 9502720 | tf_op jit(solution)/shard_map/dot_general | solution.py:101
  434.8 28.5 %reduce-scatter.2.cloned.1.call-done = f32[160,640]{1,0:T(8,128)} async-done(((f32[640,640]{1,0:T(8,128)}), f32[160,640]{1,0:T(8,128)}) %reduce-scatter.2.cloned.1.call-update) | async-done | bytes 409616 | tf_op jit(solution)/shard_map/reduce_scatter | solution.py:100
  464.6 74.2 %all-reduce.3.cloned.1.call-done = f32[160,640]{1,0:T(8,128)} async-done(((f32[160,640]{1,0:T(8,128)}), f32[160,640]{1,0:T(8,128)}) %all-reduce.3.cloned.1.call-update) | async-done | bytes 409616
  538.8 1.5 constant_dynamic-slice_fusion
  (65 shorter events, 3.9 us)
Async XLA Ops:
  13.0 7.5 %copy-start.12 = (s32[8]{0:T(128)S(1)}, s32[8]{0:T(128)}, u32[]{:S(2)}) copy-start(s32[8]{0:T(128)} %param.7) | copy-start | bytes 100
  13.0 9.4 %copy-start.13 = (s32[1,3]{1,0:T(1,128)S(1)}, s32[1,3]{1,0:T(1,128)}, u32[]{:S(2)}) copy-start(s32[1,3]{1,0:T(1,128)} %param.11) | copy-start | bytes 40
  13.0 9.4 %copy-start.9 = (bf16[1,3,4096]{2,1,0:T(4,128)(2,1)S(1)}, bf16[1,3,4096]{2,1,0:T(4,128)(2,1)}, u32[]{:S(2)}) copy-start(bf16[1,3,4096]{2,1,0:T(4,128)(2,1)} %param.10) | copy-start | bytes 73732
  13.0 9.4 %copy-start.10 = (bf16[1,3,4096]{2,1,0:T(4,128)(2,1)S(1)}, bf16[1,3,4096]{2,1,0:T(4,128)(2,1)}, u32[]{:S(2)}) copy-start(bf16[1,3,4096]{2,1,0:T(4,128)(2,1)} %param.9) | copy-start | bytes 73732
  13.0 14.9 %copy-start.11 = (s32[10,1,3]{0,1,2:T(1,128)S(1)}, s32[10,1,3]{0,1,2:T(1,128)}, u32[]{:S(2)}) copy-start(s32[10,1,3]{0,1,2:T(1,128)} %param.8) | copy-start | bytes 364
  13.1 112.3 %all-to-all-start = ((bf16[20,8,3,4096]{3,0,2,1:T(8,128)(2,1)}), bf16[20,8,3,4096]{3,0,2,1:T(8,128)(2,1)}, u32[]{:S(2)}, u32[]{:S(2)}) async-start(bf16[20,8,3,4096]{3,0,2,1:T(8,128)(2,1)} %copy.128), calls=%async_computation | async-start | bytes 9437184 | tf_op jit(solution)/shard_map/all_to_all | solution.py:80
  22.6 37.2 %collective-permute-start = (bf16[1,3,4096]{2,1,0:T(4,128)(2,1)S(1)}, bf16[1,3,4096]{2,1,0:T(4,128)(2,1)S(1)}, u32[]{:S(2)}, u32[]{:S(2)}) collective-permute-start(bf16[1,3,4096]{2,1,0:T(4,128)(2,1)S(1)} %get-tuple-element.23), channel_id=1, source_target_pairs={{0,1},{1,2},{2,3},{3,4},{4,5},{5,6},{6,7},{8,9},{9,10},{10,11},{11... | collective-permute-start | bytes 73736 | tf_op jit(solution)/shard_map/ppermute | solution.py:17
  26.5 33.5 %collective-permute-start.1 = (bf16[1,3,4096]{2,1,0:T(4,128)(2,1)S(1)}, bf16[1,3,4096]{2,1,0:T(4,128)(2,1)S(1)}, u32[]{:S(2)}, u32[]{:S(2)}) collective-permute-start(bf16[1,3,4096]{2,1,0:T(4,128)(2,1)S(1)} %get-tuple-element.23), channel_id=1, source_target_pairs={{1,0},{2,1},{3,2},{4,3},{5,4},{6,5},{7,6},{9,8},{10,9},{11,10},{12... | collective-permute-start | bytes 73736 | tf_op jit(solution)/shard_map/ppermute | solution.py:20
  145.6 171.1 %collective-permute-start.2 = (bf16[160,1,3,4096]{3,0,2,1:T(8,128)(2,1)}, bf16[160,1,3,4096]{3,0,2,1:T(8,128)(2,1)}, u32[]{:S(2)}, u32[]{:S(2)}) collective-permute-start(bf16[160,1,3,4096]{3,0,2,1:T(8,128)(2,1)} %and_select_fusion), channel_id=1, source_target_pairs={{0,1},{1,2},{2,3},{3,4},{4,5},{5,6},{6,7},{8,9},{9,10},{10,11},{11... | collective-permute-start | bytes 11796488 | tf_op jit(solution)/shard_map/ppermute | solution.py:17
  150.5 172.5 %collective-permute-start.3 = (bf16[160,1,3,4096]{3,0,2,1:T(8,128)(2,1)}, bf16[160,1,3,4096]{3,0,2,1:T(8,128)(2,1)}, u32[]{:S(2)}, u32[]{:S(2)}) collective-permute-start(bf16[160,1,3,4096]{3,0,2,1:T(8,128)(2,1)} %and_select_fusion), channel_id=1, source_target_pairs={{1,0},{2,1},{3,2},{4,3},{5,4},{6,5},{7,6},{9,8},{10,9},{11,10},{12... | collective-permute-start | bytes 11796488 | tf_op jit(solution)/shard_map/ppermute | solution.py:20
  183.8 1.6 copy-start.3
  185.3 1.6 copy-start.4
  218.5 1.6 copy-start.5
  248.1 5.4 copy-start
  248.1 131.0 %all-to-all-start.1 = ((bf16[160,4,3072]{2,0,1:T(8,128)(2,1)}), bf16[160,4,3072]{2,0,1:T(8,128)(2,1)}, u32[]{:S(2)}, u32[]{:S(2)}) async-start(bf16[160,4,3072]{2,0,1:T(8,128)(2,1)} %copy.140), calls=%async_computation.1 | async-start | bytes 7864320 | tf_op jit(solution)/shard_map/all_to_all | solution.py:97
  253.3 210.0 %reduce-scatter.2.cloned.1.call-start = ((), (), s32[]{:S(2)}) async-start(), calls=%async_computation.4 | async-start | bytes 2048000 | tf_op jit(solution)/shard_map/reduce_scatter | solution.py:100
  253.5 4.9 copy-start.1
  258.4 4.8 copy-start.2
  347.9 3.9 copy-start.6
  357.9 4.0 copy-start.7
  357.9 4.0 copy-start.8
  428.2 35.2 %copy-start.14 = (u32[32]{0:T(128)S(1)}, u32[32]{0:T(128)}, u32[]{:S(2)}) copy-start(u32[32]{0:T(128)} %constant.24) | copy-start | bytes 388
  434.8 104.0 %all-reduce.3.cloned.1.call-start = ((), (), s32[]{:S(2)}) async-start(), calls=%async_computation.5 | async-start | bytes 819200
Sparse Core Ops, SparseCore 0:
  434.9 28.3 reduce-scatter.1
  466.7 72.0 all-reduce.2
where the time goes:
time: 555 us; the launch traced here: 547 us
  waiting for transfers between devices  247 us (45%)
  local copies, waits for them, and re-layouts  146 us (26%)
  matrix products  51.6 us (9%)
  blocking collectives  49.1 us (9%)
  starting transfers between devices  24.8 us (4%)
  between operations  14.6 us (3%)
  other arithmetic  13.9 us (3%)
    ppermute x2, waiting for transfers between devices, padded(): lax.ppermute(lax.slice_in_dim(block, block.shape[dim] - width, None, axis...  79.4 us
    unnamed x3, waiting for transfers between devices  74.2 us
    all_to_all x1, waiting for transfers between devices, body(): lax.all_to_all(three_center, 'orb', split_axis=1, concat_axis=0, tiled=True)  65.1 us
    all_to_all x1, blocking collectives, body(): lax.all_to_all(second, 'aux', split_axis=1, concat_axis=0, tiled=True)  49.1 us
    another operation x16, local copies, waits for them, and re-layouts  32.3 us
    dot_general x7, matrix products, second_products(): jnp.einsum('pnls,nsv->pnlv', block, green, preferred_element_type=jnp.flo...  31.3 us
    reduce_scatter x1, waiting for transfers between devices, body(): lax.psum_scatter(lax.dot_general(left_all, right_all, (((1,), (1,)), ((),...  28.5 us
    convert_element_type x3, local copies, waits for them, and re-layouts, first_products(): total.astype(jnp.bfloat16).reshape(rows, local_blocks, BS * BS)  17.9 us
  transfers between devices with their start and end apart: 8, of which 5 were waited for; matrix products, arithmetic and copies ran while one was open for 29% of the time, Pallas kernels for 0%

commit v1 on v0

--- a/solution.py
+++ b/solution.py
@@ -77,7 +77,13 @@
 
 
 def body(three_center, atom_size, tensor_pattern, green_occ, green_virt, green_pattern):
-    regrouped = lax.all_to_all(three_center, "orb", split_axis=1, concat_axis=0, tiled=True)
+    _obtain_sizes = lambda mat, axis_id, dim_at, along_dim: jnp.concatenate(
+        jax.lax.all_to_all(
+            jnp.stack(jnp.split(mat, jax.lax.axis_size(axis_id), dim_at), axis=0), axis_id, 0, 0
+        ),
+        along_dim,
+    )
+    regrouped = _obtain_sizes(three_center, "orb", 1, 0)
     local_blocks = regrouped.shape[1]
     first_block = lax.axis_index("orb") * local_blocks
     inside, pair_ok = block_masks(atom_size, first_block, local_blocks)

time: 555 us -> 581 us (1.047)
  local copies, waits for them, and re-layouts: 146 us -> 167 us
    split x0 -> x1, local copies, waits for them, and re-layouts: none -> 18.3 us  [body(): jnp.split(mat, jax.lax.axis_size(axis_id), dim_at)]
    reshape x0 -> x1, local copies, waits for them, and re-layouts: none -> 6.07 us  [body(): jnp.concatenate(jax.lax.all_to_all(jnp.stack(jnp.split(mat, jax.lax.axis_...]
    all_to_all x2 -> x1, local copies, waits for them, and re-layouts: 11.1 us -> 5.14 us  [body(): jax.lax.all_to_all(jnp.stack(jnp.split(mat, jax.lax.axis_size(axis_id), d...]
    another operation x16 -> x17, local copies, waits for them, and re-layouts: 32.3 us -> 34.2 us
    unnamed x34 -> x40, local copies, waits for them, and re-layouts: 11.4 us -> 12.6 us
  transfers between devices with their start and end apart: 8 -> 8, of which waited for: 5 -> 5; matrix products, arithmetic and copies ran while one was open for 29% -> 28% of each run, Pallas kernels for 0% -> 0%
where the time goes in v1:
time: 581 us; the launch traced here: 570 us
  waiting for transfers between devices  246 us (42%)
  local copies, waits for them, and re-layouts  167 us (29%)
  matrix products  54.6 us (9%)
  blocking collectives  49.1 us (8%)
  starting transfers between devices  24.7 us (4%)
  between operations  14.6 us (3%)
  other arithmetic  13.8 us (2%)
    ppermute x2, waiting for transfers between devices, padded(): lax.ppermute(lax.slice_in_dim(block, block.shape[dim] - width, None, axis...  78.6 us
    unnamed x3, waiting for transfers between devices  74.2 us
    all_to_all x1, waiting for transfers between devices, body(): jax.lax.all_to_all(jnp.stack(jnp.split(mat, jax.lax.axis_size(axis_id), d...  64.5 us
    all_to_all x1, blocking collectives, body(): lax.all_to_all(second, 'aux', split_axis=1, concat_axis=0, tiled=True)  49.1 us
    another operation x16, local copies, waits for them, and re-layouts  32.8 us
    dot_general x7, matrix products, second_products(): jnp.einsum('pnls,nsv->pnlv', block, green, preferred_element_type=jnp.flo...  31.2 us
    reduce_scatter x1, waiting for transfers between devices, body(): lax.psum_scatter(lax.dot_general(left_all, right_all, (((1,), (1,)), ((),...  29.1 us
    split x1, local copies, waits for them, and re-layouts, body(): jnp.split(mat, jax.lax.axis_size(axis_id), dim_at)  18.3 us
  transfers between devices with their start and end apart: 8, of which 5 were waited for; matrix products, arithmetic and copies ran while one was open for 28% of the time, Pallas kernels for 0%

profile of v1, /device:TPU:0, one launch (start us, length us, event | category | flops | bytes accessed | tf_op | source)
XLA Modules:
  0.0 570.3 jit_solution(8787560449829070392)
XLA Ops:
  6.5 18.3 %fusion.34 = (bf16[20,1,3,4096]{3,1,2,0:T(2,128)(2,1)S(1)}, bf16[20,1,3,4096]{3,1,2,0:T(2,128)(2,1)S(1)}, bf16[20,1,3,4096]{3,1,2,0:T(2,128)(2,1)S(1)}, bf16[20,...) fusion(bf16[20,8,3,4096]{3,1,2,0:T(8,128)(2,1)} %param.6), kind=kLoop, calls=%fused_computation.73 | loop fusion | bytes 7864320 | tf_op jit(solution)/shard_map/split | solution.py:82
  26.2 1.4 fusion.15
  27.5 1.4 fusion.14
  28.9 1.4 fusion.13
  30.3 1.4 fusion.12
  31.6 1.4 fusion.11
  33.0 1.4 fusion.10
  34.4 1.4 fusion.9
  35.7 7.5 %all-to-all-start = ((bf16[8,20,1,3,4096]{4,1,3,2,0:T(8,128)(2,1)}), bf16[8,20,1,3,4096]{4,1,3,2,0:T(8,128)(2,1)}, u32[]{:S(2)}, u32[]{:S(2)}) async-start(bf16[8,20,1,3,4096]{4,1,3,2,0:T(8,128)(2,1)} %fusion.9), calls=%async_computation | async-start | bytes 9437184 | tf_op jit(solution)/shard_map/all_to_all | solution.py:81
  45.3 3.9 collective-permute-start
  51.6 30.9 %collective-permute-done = bf16[1,3,4096]{2,1,0:T(4,128)(2,1)S(1)} collective-permute-done((bf16[1,3,4096]{2,1,0:T(4,128)(2,1)S(1)}, bf16[1,3,4096]{2,1,0:T(4,128)(2,1)S(1)}, u32[]{:S(2)}, u32[]{:S(2)}) %collective-permute-start) | collective-permute-done | bytes 24608 | tf_op jit(solution)/shard_map/ppermute | solution.py:17
  83.6 64.5 %all-to-all-done = bf16[8,20,1,3,4096]{4,1,3,2,0:T(8,128)(2,1)} async-done(((bf16[8,20,1,3,4096]{4,1,3,2,0:T(8,128)(2,1)}), bf16[8,20,1,3,4096]{4,1,3,2,0:T(8,128)(2,1)}, u32[]{:S(2)}, u32[]{:S(2)}) %all-to-all-start) | async-done | bytes 3932192 | tf_op jit(solution)/shard_map/all_to_all | solution.py:81
  148.1 5.1 copy.135
  153.2 6.1 %reshape.443 = bf16[160,1,3,4096]{3,0,2,1:T(8,128)(2,1)} reshape(bf16[8,20,1,3,4096]{4,1,0,3,2:T(8,128)(2,1)} %copy.135) | data formatting | bytes 7864320 | tf_op jit(solution)/shard_map/reshape | solution.py:80
  159.3 5.5 and_select_fusion
  164.7 3.5 fusion.33
  168.3 5.0 collective-permute-start.2
  173.3 1.5 collective-permute-start.3
  174.7 4.8 reshape.446
  179.5 3.9 reshape.444
  183.4 5.6 copy.137
  189.0 6.6 %copy.136 = bf16[160,64,64]{0,1,2:T(8,128)(2,1)} copy(bf16[160,64,64]{2,1,0:T(8,128)(2,1)} %reshape.444) | data formatting | bytes 2621440 | tf_op jit(solution)/shard_map/reshape.24
  196.4 2.6 fusion.38
  199.0 2.7 fusion.37
  201.7 2.0 fusion.7
  203.8 3.9 reshape.451
  207.6 6.2 %copy.138 = bf16[160,1,64,64]{3,2,0,1:T(8,128)(2,1)} copy(bf16[160,1,64,64]{0,2,3,1:T(8,128)(2,1)} %fusion.7) | data formatting | bytes 2621440 | tf_op jit(solution)/shard_map/convert_element_type | solution.py:56
  213.9 4.6 reshape.448
  218.5 6.6 %copy.141 = bf16[160,64,64]{0,1,2:T(8,128)(2,1)} copy(bf16[160,64,64]{2,1,0:T(8,128)(2,1)} %reshape.451) | data formatting | bytes 2621440 | tf_op jit(solution)/shard_map/reshape.36
  225.1 6.1 %fusion.6 = bf16[160,1,64,64]{0,2,3,1:T(8,128)(2,1)} fusion(f32[160,64,64]{0,2,1:T(8,128)} %fusion.37, f32[160,64,64]{0,2,1:T(8,128)} %fusion.38, bf16[64,64,1]{1,0,2:T(8,128)(2,1)S(1)} %reshape.471, bf16[160,64,64]{0,1,2:T(8,128)(2,1)} %copy.141), kind=kOutput, calls=%fused_computation.15 | convolution fusion | flops 85852160 | bytes 7872512 | tf_op jit(solution)/shard_map/nlm,pnmv->pnlv/dot_general | solution.py:53
  231.2 6.4 %copy.142 = bf16[160,1,64,64]{3,2,0,1:T(8,128)(2,1)} copy(bf16[160,1,64,64]{0,2,3,1:T(8,128)(2,1)} %fusion.6) | data formatting | bytes 2621440 | tf_op jit(solution)/shard_map/convert_element_type | solution.py:56
  237.6 4.6 reshape.453
  243.8 2.0 fusion.8
  245.8 5.3 copy.145
  251.2 2.9 reshape.456
  254.0 3.5 pad_maximum_fusion
  257.5 9.0 %all_to_all.32 = bf16[160,4,3072]{2,1,0:T(4,128)(2,1)} reshape(bf16[160,1,12288]{2,0,1:T(8,128)(2,1)} %pad_maximum_fusion) | data formatting | bytes 7864320 | tf_op jit(solution)/shard_map/all_to_all | solution.py:103
  266.5 5.2 copy.146
  271.6 5.1 all-to-all-start.1
  277.2 4.7 fusion.2
  282.0 4.8 fusion.4
  286.8 4.8 fusion
  291.6 47.7 %collective-permute-done.2 = bf16[160,1,3,4096]{3,0,2,1:T(8,128)(2,1)} collective-permute-done((bf16[160,1,3,4096]{3,0,2,1:T(8,128)(2,1)}, bf16[160,1,3,4096]{3,0,2,1:T(8,128)(2,1)}, u32[]{:S(2)}, u32[]{:S(2)}) %collective-permute-start.2) | collective-permute-done | bytes 3932192 | tf_op jit(solution)/shard_map/ppermute | solution.py:17
  339.3 3.0 fusion.31
  342.3 3.2 copy.151
  345.6 3.5 fusion.32
  349.1 2.7 fusion.25
  351.7 3.1 copy.155
  354.8 5.5 add_convert_fusion.1
  360.4 3.8 copy.162
  364.2 1.8 copy.147
  366.0 4.3 add_convert_fusion.2
  370.4 3.8 copy.161
  374.2 1.8 copy.159
  376.0 4.3 add_convert_fusion
  380.4 3.9 copy.163
  384.3 3.1 pad_maximum_fusion.1
  387.4 9.0 %all_to_all.36 = bf16[160,4,3072]{2,1,0:T(4,128)(2,1)} reshape(bf16[160,1,12288]{2,0,1:T(8,128)(2,1)} %pad_maximum_fusion.1) | data formatting | bytes 7864320 | tf_op jit(solution)/shard_map/all_to_all | solution.py:104
  396.3 5.2 copy.164
  401.5 49.1 %all_to_all.43 = bf16[160,4,3072]{2,0,1:T(8,128)(2,1)S(1)} all-to-all(bf16[160,4,3072]{2,0,1:T(8,128)(2,1)} %copy.164), channel_id=1, replica_groups=mesh['aux'=4,'orb'=8] {'aux'}, dimensions={1} | all-to-all | bytes 7864320 | tf_op jit(solution)/shard_map/all_to_all | solution.py:104
  450.6 6.6 %fusion.35 = f32[640,640]{1,0:T(8,128)} fusion(bf16[640,3072]{1,0:T(8,128)(2,1)} %bitcast.16, bf16[640,3072]{1,0:T(8,128)(2,1)S(1)} %bitcast.157), kind=kOutput, calls=%fused_computation.74 | convolution fusion | flops 2516582400 | bytes 9502720 | tf_op jit(solution)/shard_map/dot_general | solution.py:107
  457.2 29.1 %reduce-scatter.2.cloned.1.call-done = f32[160,640]{1,0:T(8,128)} async-done(((f32[640,640]{1,0:T(8,128)}), f32[160,640]{1,0:T(8,128)}) %reduce-scatter.2.cloned.1.call-update) | async-done | bytes 409616 | tf_op jit(solution)/shard_map/reduce_scatter | solution.py:106
  487.6 74.2 %all-reduce.3.cloned.1.call-done = f32[160,640]{1,0:T(8,128)} async-done(((f32[160,640]{1,0:T(8,128)}), f32[160,640]{1,0:T(8,128)}) %all-reduce.3.cloned.1.call-update) | async-done | bytes 409616
  561.8 1.5 constant_dynamic-slice_fusion
  (73 shorter events, 10.3 us)
Async XLA Ops:
  35.7 7.5 %copy-start.12 = (s32[8]{0:T(128)S(1)}, s32[8]{0:T(128)}, u32[]{:S(2)}) copy-start(s32[8]{0:T(128)} %param.7) | copy-start | bytes 100
  35.7 9.4 %copy-start.13 = (s32[1,3]{1,0:T(1,128)S(1)}, s32[1,3]{1,0:T(1,128)}, u32[]{:S(2)}) copy-start(s32[1,3]{1,0:T(1,128)} %param.11) | copy-start | bytes 40
  35.7 9.4 %copy-start.9 = (bf16[1,3,4096]{2,1,0:T(4,128)(2,1)S(1)}, bf16[1,3,4096]{2,1,0:T(4,128)(2,1)}, u32[]{:S(2)}) copy-start(bf16[1,3,4096]{2,1,0:T(4,128)(2,1)} %param.10) | copy-start | bytes 73732
  35.7 9.4 %copy-start.10 = (bf16[1,3,4096]{2,1,0:T(4,128)(2,1)S(1)}, bf16[1,3,4096]{2,1,0:T(4,128)(2,1)}, u32[]{:S(2)}) copy-start(bf16[1,3,4096]{2,1,0:T(4,128)(2,1)} %param.9) | copy-start | bytes 73732
  35.7 14.9 %copy-start.11 = (s32[10,1,3]{0,1,2:T(1,128)S(1)}, s32[10,1,3]{0,1,2:T(1,128)}, u32[]{:S(2)}) copy-start(s32[10,1,3]{0,1,2:T(1,128)} %param.8) | copy-start | bytes 364
  35.7 112.3 %all-to-all-start = ((bf16[8,20,1,3,4096]{4,1,3,2,0:T(8,128)(2,1)}), bf16[8,20,1,3,4096]{4,1,3,2,0:T(8,128)(2,1)}, u32[]{:S(2)}, u32[]{:S(2)}) async-start(bf16[8,20,1,3,4096]{4,1,3,2,0:T(8,128)(2,1)} %fusion.9), calls=%async_computation | async-start | bytes 9437184 | tf_op jit(solution)/shard_map/all_to_all | solution.py:81
  45.3 37.2 %collective-permute-start = (bf16[1,3,4096]{2,1,0:T(4,128)(2,1)S(1)}, bf16[1,3,4096]{2,1,0:T(4,128)(2,1)S(1)}, u32[]{:S(2)}, u32[]{:S(2)}) collective-permute-start(bf16[1,3,4096]{2,1,0:T(4,128)(2,1)S(1)} %get-tuple-element.31), channel_id=1, source_target_pairs={{0,1},{1,2},{2,3},{3,4},{4,5},{5,6},{6,7},{8,9},{9,10},{10,11},{11... | collective-permute-start | bytes 73736 | tf_op jit(solution)/shard_map/ppermute | solution.py:17
  49.2 34.1 %collective-permute-start.1 = (bf16[1,3,4096]{2,1,0:T(4,128)(2,1)S(1)}, bf16[1,3,4096]{2,1,0:T(4,128)(2,1)S(1)}, u32[]{:S(2)}, u32[]{:S(2)}) collective-permute-start(bf16[1,3,4096]{2,1,0:T(4,128)(2,1)S(1)} %get-tuple-element.31), channel_id=1, source_target_pairs={{1,0},{2,1},{3,2},{4,3},{5,4},{6,5},{7,6},{9,8},{10,9},{11,10},{12... | collective-permute-start | bytes 73736 | tf_op jit(solution)/shard_map/ppermute | solution.py:20
  168.3 171.1 %collective-permute-start.2 = (bf16[160,1,3,4096]{3,0,2,1:T(8,128)(2,1)}, bf16[160,1,3,4096]{3,0,2,1:T(8,128)(2,1)}, u32[]{:S(2)}, u32[]{:S(2)}) collective-permute-start(bf16[160,1,3,4096]{3,0,2,1:T(8,128)(2,1)} %and_select_fusion), channel_id=1, source_target_pairs={{0,1},{1,2},{2,3},{3,4},{4,5},{5,6},{6,7},{8,9},{9,10},{10,11},{11... | collective-permute-start | bytes 11796488 | tf_op jit(solution)/shard_map/ppermute | solution.py:17
  173.3 172.3 %collective-permute-start.3 = (bf16[160,1,3,4096]{3,0,2,1:T(8,128)(2,1)}, bf16[160,1,3,4096]{3,0,2,1:T(8,128)(2,1)}, u32[]{:S(2)}, u32[]{:S(2)}) collective-permute-start(bf16[160,1,3,4096]{3,0,2,1:T(8,128)(2,1)} %and_select_fusion), channel_id=1, source_target_pairs={{1,0},{2,1},{3,2},{4,3},{5,4},{6,5},{7,6},{9,8},{10,9},{11,10},{12... | collective-permute-start | bytes 11796488 | tf_op jit(solution)/shard_map/ppermute | solution.py:20
  196.3 2.7 copy-start.3
  196.3 2.6 copy-start.8
  242.2 1.6 copy-start.4
  271.6 5.5 copy-start
  271.6 129.9 %all-to-all-start.1 = ((bf16[160,4,3072]{2,0,1:T(8,128)(2,1)}), bf16[160,4,3072]{2,0,1:T(8,128)(2,1)}, u32[]{:S(2)}, u32[]{:S(2)}) async-start(bf16[160,4,3072]{2,0,1:T(8,128)(2,1)} %copy.146), calls=%async_computation.1 | async-start | bytes 7864320 | tf_op jit(solution)/shard_map/all_to_all | solution.py:103
  276.7 209.6 %reduce-scatter.2.cloned.1.call-start = ((), (), s32[]{:S(2)}) async-start(), calls=%async_computation.4 | async-start | bytes 2048000 | tf_op jit(solution)/shard_map/reduce_scatter | solution.py:106
  277.2 4.7 copy-start.1
  282.0 4.8 copy-start.2
  366.0 8.1 %copy-start.5 = (bf16[160,1,1,4096]{3,0,2,1:T(8,128)(2,1)S(1)}, bf16[160,1,1,4096]{3,0,2,1:T(8,128)(2,1)}, u32[]{:S(2)}) copy-start(bf16[160,1,1,4096]{3,0,2,1:T(8,128)(2,1)} %get-tuple-element.18) | copy-start | bytes 3932164
  376.0 8.3 %copy-start.6 = (bf16[160,1,4096]{2,0,1:T(8,128)(2,1)S(1)}, bf16[160,1,4096]{2,0,1:T(8,128)(2,1)}, u32[]{:S(2)}) copy-start(bf16[160,1,4096]{2,0,1:T(8,128)(2,1)} %copy.162) | copy-start | bytes 3932164
  380.4 3.9 copy-start.7
  450.6 35.8 %copy-start.14 = (u32[32]{0:T(128)S(1)}, u32[32]{0:T(128)}, u32[]{:S(2)}) copy-start(u32[32]{0:T(128)} %constant.24) | copy-start | bytes 388
  457.2 104.6 %all-reduce.3.cloned.1.call-start = ((), (), s32[]{:S(2)}) async-start(), calls=%async_computation.5 | async-start | bytes 819200
Sparse Core Ops, SparseCore 0:
  457.3 28.9 reduce-scatter.1
  489.7 71.9 all-reduce.2
